TPU v7x, 512 devices: a whole 4x8x8 slice. The times are simulated.
512 devices in a mesh: dp: 32 (over z, x), expert: 16 (over y, core).
Axes of the slice: x: 4, y: 8, z: 8, core: 2. Of those that a mesh axis runs over, the one named last changes fastest.
Arguments:
- tokens: bfloat16 [100352, 1024], P(('dp', 'expert')), may hold values from -6 to 6
- route_weight: bfloat16 [100352], P(('dp', 'expert')), may hold values from 0.29882812 to 1
- expert_ids: int32 [100352, 1], P(('dp', 'expert')), may hold values from 0 to 15; in each aligned block of 196 rows (0 to 195, 196 to 391, ...) at most 24 rows name the same one
- visible: int32 [2048, 49], P(('dp', 'expert')), may hold values from 0 to 195, as said below
- owner_map: int32 [2048], P(('dp', 'expert')), may hold values from 0 to 15, as said below
- norm_gain: float32 [1024], replicated, may hold values from 0.5 to 1.5
- expert_in: bfloat16 [16, 2048, 1024], P('expert', 'dp'), may hold values from -0.1875 to 0.1875
- expert_out: bfloat16 [16, 2048, 1024], P('expert', 'dp'), may hold values from -0.125 to 0.125
- final_gain: float32 [1024], replicated, may hold values from 0.5 to 1.5
- embed_weight: bfloat16 [1024, 512], replicated, may hold values from -0.1875 to 0.1875
- mask_token: bfloat16 [512], replicated, may hold values from -4 to 4
- decoder_pos: bfloat16 [196, 512], replicated, may hold values from -3 to 3
- decoder_gain: float32 [512], replicated, may hold values from 0.5 to 1.5
- attention_in: bfloat16 [512, 1536], replicated
- attention_out: bfloat16 [512, 512], replicated, may hold values from -0.25 to 0.25
Outputs:
- decoded_grid: bfloat16 [2048, 196, 512], P(('dp', 'expert'))
Inputs may be any that keep to these rules, and one draw needn't show every extreme that they name: `expert_ids`: in each aligned block of 196 rows (the tokens of one device) no expert is named by more than 24 rows. `visible`: each row names 49 different positions. `owner_map`: the 4 images of an aligned block (one device) share one owner; in each aligned block of 64 images the 16 blocks have different owners.
All inputs are finite; a program needn't handle non-finite values.
Results may differ from a plain program's by a relative error of at most 0.009.
Values may be sent and summed in bfloat16 or wider, within the bound.
A program may use at most 64 MiB of HBM per device.

v0:
```python
import jax
import jax.numpy as jnp
from jax import lax
from jax.sharding import PartitionSpec as P

D = 1024
HEADS = 16
HEAD_DIM = 32
DD = 512
GRID = 196
VIS = 49
EPSILON = 1e-06


def layer_norm(values, factor):
    values = values.astype(jnp.float32)
    centered = values - jnp.mean(values, axis=-1, keepdims=True)
    variance = jnp.mean(centered * centered, axis=-1, keepdims=True)
    return centered * lax.rsqrt(variance + EPSILON) * factor


def slot_table(token_expert, experts, capacity):
    onehot = (token_expert[:, None] == jnp.arange(experts, dtype=jnp.int32)[None, :]).astype(
        jnp.int32
    )
    earlier = jnp.sum((jnp.cumsum(onehot, axis=0) - onehot) * onehot, axis=1)
    slot_index = token_expert * capacity + earlier
    return (slot_index[:, None] == jnp.arange(experts * capacity, dtype=jnp.int32)[None, :]).astype(
        jnp.bfloat16
    )


def embed_rows(merged, final_gain, embed_weight):
    final_normed = layer_norm(merged, final_gain).astype(jnp.bfloat16)
    return jnp.dot(final_normed, embed_weight, preferred_element_type=jnp.float32).astype(
        jnp.bfloat16
    )


def per_device(
    tokens,
    route_weight,
    expert_ids,
    visible,
    owner_map,
    norm_gain,
    expert_in,
    expert_out,
    final_gain,
    embed_weight,
    mask_token,
    decoder_pos,
    decoder_gain,
    attention_in,
    attention_out,
):
    groups = lax.axis_size("expert")
    tok_dev = tokens.shape[0]
    img_dev = visible.shape[0]
    exp_dev = expert_in.shape[0]
    experts = exp_dev * groups
    capacity = 2 * tok_dev // experts
    own_index = lax.axis_index("expert")
    token_expert = expert_ids[:, 0]
    all_ids, all_visible, all_owner = (
        lax.all_gather(token_expert, "expert", axis=0, tiled=True),
        lax.all_gather(visible, "expert", axis=0, tiled=True),
        lax.all_gather(owner_map, "expert", axis=0, tiled=True),
    )
    placing = slot_table(token_expert, experts, capacity)
    send_rows = jnp.dot(placing.T, tokens, preferred_element_type=jnp.float32).astype(jnp.bfloat16)
    send_weight = jnp.einsum(
        "ts,t->s", placing, route_weight, preferred_element_type=jnp.float32
    ).astype(jnp.bfloat16)
    arrived_rows, arrived_weight = (
        lax.all_to_all(
            send_rows.reshape(groups, exp_dev * capacity, D),
            "expert",
            split_axis=0,
            concat_axis=0,
            tiled=True,
        ),
        lax.all_to_all(
            send_weight.reshape(groups, exp_dev * capacity),
            "expert",
            split_axis=0,
            concat_axis=0,
            tiled=True,
        ),
    )
    expert_rows = (
        arrived_rows.reshape(groups, exp_dev, capacity, D)
        .transpose(1, 0, 2, 3)
        .reshape(exp_dev, groups * capacity, D)
    )
    expert_weight = (
        arrived_weight.reshape(groups, exp_dev, capacity)
        .transpose(1, 0, 2)
        .reshape(exp_dev, groups * capacity)
    )
    normed = layer_norm(expert_rows, norm_gain).astype(jnp.bfloat16)
    piece_in = lax.all_gather(expert_in, "dp", axis=1, tiled=True)
    piece_out = lax.all_gather(expert_out, "dp", axis=1, tiled=True)
    hidden = jax.nn.gelu(
        jnp.einsum("esd,efd->esf", normed, piece_in, preferred_element_type=jnp.float32)
    ).astype(jnp.bfloat16)
    update = jnp.einsum("esf,efd->esd", hidden, piece_out, preferred_element_type=jnp.float32)
    merged = (
        expert_rows.astype(jnp.float32) + expert_weight.astype(jnp.float32)[:, :, None] * update
    ).astype(jnp.bfloat16)
    source_owner = all_owner.reshape(groups, img_dev)[:, 0]
    to_owner = (source_owner[None, :] == jnp.arange(groups, dtype=jnp.int32)[:, None]).astype(
        jnp.bfloat16
    )
    source = jnp.sum(
        jnp.arange(groups, dtype=jnp.int32) * (source_owner == own_index).astype(jnp.int32)
    )
    source_ids = lax.dynamic_slice_in_dim(all_ids, source * tok_dev, tok_dev)
    source_visible = lax.dynamic_slice_in_dim(all_visible, source * img_dev, img_dev)
    source_table = slot_table(source_ids, experts, capacity)
    payload = (
        merged.reshape(exp_dev, groups, capacity, D)
        .transpose(1, 0, 2, 3)
        .reshape(groups, exp_dev * capacity, D)
    )
    outgoing = jnp.einsum(
        "os,scw->ocw", to_owner, payload, preferred_element_type=jnp.float32
    ).astype(jnp.bfloat16)
    arrived = lax.all_to_all(outgoing, "expert", split_axis=0, concat_axis=0, tiled=True)
    own_rows = jnp.dot(
        source_table, arrived.reshape(experts * capacity, D), preferred_element_type=jnp.float32
    ).astype(jnp.bfloat16)
    embedded = embed_rows(own_rows, final_gain, embed_weight)
    image_rows = embedded.reshape(img_dev, 1, VIS, DD)
    image_places = source_visible.reshape(img_dev, 1, VIS)

    def decode_image(operands):
        rows_one, places_one = operands
        position_hit = places_one[:, :, None] == jnp.arange(GRID, dtype=jnp.int32)[None, None, :]
        covered = jnp.any(position_hit, axis=1)
        placed = jnp.einsum(
            "ivg,ivd->igd",
            position_hit.astype(jnp.bfloat16),
            rows_one,
            preferred_element_type=jnp.float32,
        )
        canvas = jnp.where(
            covered[:, :, None], placed, mask_token.astype(jnp.float32)[None, None, :]
        )
        initial = canvas + decoder_pos.astype(jnp.float32)[None]
        dec_normed = layer_norm(initial, decoder_gain).astype(jnp.bfloat16)
        projected = jnp.dot(
            dec_normed.reshape(GRID, DD), attention_in, preferred_element_type=jnp.float32
        ).astype(jnp.bfloat16)
        projected = projected.reshape(1, GRID, 3, HEADS, HEAD_DIM)
        queries = projected[:, :, 0]
        key_rows = projected[:, :, 1]
        value_rows = projected[:, :, 2]
        scores = jnp.einsum(
            "iqhc,ikhc->ihqk", queries, key_rows, preferred_element_type=jnp.float32
        ) * HEAD_DIM ** (-0.5)
        highest = jnp.max(scores, axis=-1, keepdims=True)
        raised = jnp.exp(scores - highest)
        weights = (raised / jnp.sum(raised, axis=-1, keepdims=True)).astype(jnp.bfloat16)
        mixed = jnp.einsum(
            "ihqk,ikhc->iqhc", weights, value_rows, preferred_element_type=jnp.float32
        ).astype(jnp.bfloat16)
        update_out = jnp.dot(
            mixed.reshape(GRID, DD), attention_out, preferred_element_type=jnp.float32
        )
        return (initial + update_out.reshape(1, GRID, DD)).astype(jnp.bfloat16)

    decoded = lax.map(decode_image, (image_rows, image_places))
    return decoded.reshape(img_dev, GRID, DD)


def solution(mesh):
    return jax.shard_map(
        per_device,
        mesh=mesh,
        in_specs=(
            P(("dp", "expert"), None),
            P(("dp", "expert")),
            P(("dp", "expert"), None),
            P(("dp", "expert"), None),
            P(("dp", "expert")),
            P(),
            P("expert", "dp", None),
            P("expert", "dp", None),
            P(),
            P(),
            P(),
            P(),
            P(),
            P(),
            P(),
        ),
        out_specs=P(("dp", "expert"), None, None),
        check_vma=False,
    )
```

profile of v0, /device:TPU:1, one launch (start us, length us, event | category | flops | bytes accessed | tf_op | source)
XLA Modules:
  0.0 293.3 jit_solution(7976622157471527330)
XLA Ops:
  12.6 10.1 %all-to-all-start.1 = ((bf16[16,1,24]{2,1,0:T(2,128)(2,1)}), bf16[16,1,24]{2,1,0:T(2,128)(2,1)S(1)}, u32[]{:S(2)}, u32[]{:S(2)}) async-start(bf16[16,1,24]{2,1,0:T(2,128)(2,1)} %all_to_all.16), calls=%async_computation.1 | async-start | bytes 16384 | tf_op jit(solution)/shard_map/all_to_all | solution.py:83
  22.6 2.4 convolution_convert_fusion.2
  25.0 4.7 %all-to-all-done.1 = bf16[16,1,24]{2,1,0:T(2,128)(2,1)S(1)} async-done(((bf16[16,1,24]{2,1,0:T(2,128)(2,1)}), bf16[16,1,24]{2,1,0:T(2,128)(2,1)S(1)}, u32[]{:S(2)}, u32[]{:S(2)}) %all-to-all-start.1) | async-done | bytes 800 | tf_op jit(solution)/shard_map/all_to_all | solution.py:83
  29.7 4.2 %all-to-all-start = ((bf16[16,24,1024]{2,1,0:T(8,128)(2,1)}), bf16[16,24,1024]{2,1,0:T(8,128)(2,1)S(1)}, u32[]{:S(2)}, u32[]{:S(2)}) async-start(bf16[16,24,1024]{2,1,0:T(8,128)(2,1)} %bitcast.22), calls=%async_computation | async-start | bytes 1572864 | tf_op jit(solution)/shard_map/all_to_all | solution.py:76
  36.9 55.7 %all-reduce.4 = (s32[64]{0:T(128)S(1)}, s32[3136]{0:T(1024)S(1)}) all-reduce(s32[64]{0:T(128)S(1)} %dynamic-update-slice, s32[3136]{0:T(1024)S(1)} %dynamic-update-slice.1), channel_id=1, replica_groups=mesh['dp'=32,'expert'=16] {'expert'}, use_global_device_ids=true, to_apply=%add.2 | all-reduce | flops 3200 | bytes 25600
  94.1 7.1 %all-gather.5.cloned.1.call-done = bf16[1,2048,1024]{2,1,0:T(8,128)(2,1)} async-done(((bf16[1,64,1024]{2,1,0:T(8,128)(2,1)}), bf16[1,2048,1024]{2,1,0:T(8,128)(2,1)}) %all-gather.5.cloned.1.call-update) | async-done | bytes 4194320 | tf_op jit(solution)/shard_map/all_gather | solution.py:102
  101.2 88.0 %all-gather.7.cloned.1.call-done = bf16[1,2048,1024]{2,1,0:T(8,128)(2,1)} async-done(((bf16[1,64,1024]{2,1,0:T(8,128)(2,1)}), bf16[1,2048,1024]{2,1,0:T(8,128)(2,1)}) %all-gather.7.cloned.1.call-update) | async-done | bytes 4194320 | tf_op jit(solution)/shard_map/all_gather | solution.py:103
  189.2 7.1 %fusion.42 = bf16[384,1024]{1,0:T(8,128)(2,1)S(1)} fusion(bf16[1,2048,1024]{2,1,0:T(8,128)(2,1)} %all-gather.7.cloned.1.call-done, bf16[384,1024]{1,0:T(8,128)(2,1)S(1)} %bitcast.150, bf16[1,2048,1024]{2,1,0:T(8,128)(2,1)} %all-gather.5.cloned.1.call-done, bf16[16,24,1024]{2,1,0:T(8,128)(2,1)S(1)} %all-to-all-done, f32[384]{0:T(512)S(1)} %reshape.421), kind=kOutput, calls=%fused_computation.55 | convolution fusion | flops 3229876224 | bytes 10749440 | tf_op jit(solution)/shard_map/esf,efd->esd/dot_general | solution.py:107
  198.3 10.9 %all-to-all-start.2 = ((bf16[16,24,1024]{2,1,0:T(8,128)(2,1)}), bf16[16,24,1024]{2,1,0:T(8,128)(2,1)S(1)}, u32[]{:S(2)}, u32[]{:S(2)}) async-start(bf16[16,24,1024]{2,1,0:T(8,128)(2,1)} %copy.52), calls=%async_computation.2 | async-start | bytes 1572864 | tf_op jit(solution)/shard_map/all_to_all | solution.py:129
  212.3 28.1 %all-gather.1 = s32[16,4,49]{2,1,0:T(4,128)S(1)} all-gather(s32[1,4,49]{2,1,0:T(4,128)S(1)} %bitcast.159), channel_id=1, replica_groups=mesh['dp'=32,'expert'=16] {'expert'}, dimensions={0}, use_global_device_ids=true | all-gather | bytes 13328 | tf_op jit(solution)/shard_map/all_gather | solution.py:67
  242.6 41.3 %while.10 = (s32[]{:T(128)}, bf16[4,1,196,512]{3,2,1,0:T(8,128)(2,1)}, s32[4,1,49]{2,1,0:T(1,128)S(1)}, bf16[4,1,49,512]{3,2,1,0:T(8,128)(2,1)}, bf16[512]{0:T(5...) while((s32[]{:T(128)}, ...), condition=%wide.region_17.18_spmd, body=%wide.region_11.17_spmd.sunk | while | flops 504361024 | bytes 12126609 | solution.py:173
  244.4 1.9 convolution_convert_fusion.6
  246.6 3.0 %fusion.93 = (f32[16,196]{1,0:T(8,128)S(1)}, f32[16,196,196]{1,2,0:T(8,128)}) fusion(bf16[1,196,3,16,32]{1,4,3,2,0:T(8,128)(2,1)S(1)} %bitcast.145), kind=kOutput, calls=%fused_computation.115.clone.1 | convolution fusion | flops 41182148 | bytes 2995456 | tf_op jit(solution)/shard_map/while/body/eval_jaxpr/sub | solution.py:163
  249.6 2.4 fusion.94
  254.7 1.9 convolution_convert_fusion.6
  256.9 3.0 %fusion.93 = (f32[16,196]{1,0:T(8,128)S(1)}, f32[16,196,196]{1,2,0:T(8,128)}) fusion(bf16[1,196,3,16,32]{1,4,3,2,0:T(8,128)(2,1)S(1)} %bitcast.145), kind=kOutput, calls=%fused_computation.115.clone.1 | convolution fusion | flops 41182148 | bytes 2995456 | tf_op jit(solution)/shard_map/while/body/eval_jaxpr/sub | solution.py:163
  259.9 2.4 fusion.94
  265.0 1.9 convolution_convert_fusion.6
  267.3 3.0 %fusion.93 = (f32[16,196]{1,0:T(8,128)S(1)}, f32[16,196,196]{1,2,0:T(8,128)}) fusion(bf16[1,196,3,16,32]{1,4,3,2,0:T(8,128)(2,1)S(1)} %bitcast.145), kind=kOutput, calls=%fused_computation.115.clone.1 | convolution fusion | flops 41182148 | bytes 2995456 | tf_op jit(solution)/shard_map/while/body/eval_jaxpr/sub | solution.py:163
  270.3 2.4 fusion.94
  275.4 1.9 convolution_convert_fusion.6
  277.6 3.0 %fusion.93 = (f32[16,196]{1,0:T(8,128)S(1)}, f32[16,196,196]{1,2,0:T(8,128)}) fusion(bf16[1,196,3,16,32]{1,4,3,2,0:T(8,128)(2,1)S(1)} %bitcast.145), kind=kOutput, calls=%fused_computation.115.clone.1 | convolution fusion | flops 41182148 | bytes 2995456 | tf_op jit(solution)/shard_map/while/body/eval_jaxpr/sub | solution.py:163
  280.6 2.4 fusion.94
  284.0 2.4 copy.67
  (110 shorter events, 26.9 us)
Async XLA Ops:
  6.5 234.9 %copy-start = (bf16[1024,512]{1,0:T(8,128)(2,1)S(1)}, bf16[1024,512]{1,0:T(8,128)(2,1)}, u32[]{:S(2)}) copy-start(bf16[1024,512]{1,0:T(8,128)(2,1)} %param.26) | copy-start | bytes 3145732
  6.5 29.8 %copy-start.4 = (s32[196,1]{0,1:T(1,128)S(1)}, s32[196,1]{0,1:T(1,128)}, u32[]{:S(2)}) copy-start(s32[196,1]{0,1:T(1,128)} %param.19) | copy-start | bytes 2356
  6.5 30.1 %copy-start.8 = (s32[4]{0:T(128)S(1)}, s32[4]{0:T(128)}, u32[]{:S(2)}) copy-start(s32[4]{0:T(128)} %param.21) | copy-start | bytes 52
  6.5 94.7 %all-gather.5.cloned.1.call-start = ((), (), s32[]{:S(2)}) async-start(), calls=%async_computation.3 | async-start | bytes 4325376 | tf_op jit(solution)/shard_map/all_gather | solution.py:102
  7.3 182.0 %all-gather.7.cloned.1.call-start = ((), (), s32[]{:S(2)}) async-start(), calls=%async_computation.4 | async-start | bytes 4325376 | tf_op jit(solution)/shard_map/all_gather | solution.py:103
  12.6 17.1 %all-to-all-start.1 = ((bf16[16,1,24]{2,1,0:T(2,128)(2,1)}), bf16[16,1,24]{2,1,0:T(2,128)(2,1)S(1)}, u32[]{:S(2)}, u32[]{:S(2)}) async-start(bf16[16,1,24]{2,1,0:T(2,128)(2,1)} %all_to_all.16), calls=%async_computation.1 | async-start | bytes 16384 | tf_op jit(solution)/shard_map/all_to_all | solution.py:83
  29.7 64.0 %copy-start.5 = (f32[1024]{0:T(1024)S(1)}, f32[1024]{0:T(1024)}, u32[]{:S(2)}) copy-start(f32[1024]{0:T(1024)} %param.22) | copy-start | bytes 12292
  29.7 63.2 %all-to-all-start = ((bf16[16,24,1024]{2,1,0:T(8,128)(2,1)}), bf16[16,24,1024]{2,1,0:T(8,128)(2,1)S(1)}, u32[]{:S(2)}, u32[]{:S(2)}) async-start(bf16[16,24,1024]{2,1,0:T(8,128)(2,1)} %bitcast.22), calls=%async_computation | async-start | bytes 1572864 | tf_op jit(solution)/shard_map/all_to_all | solution.py:76
  196.3 16.0 %copy-start.7 = (s32[4,49]{1,0:T(4,128)S(1)}, s32[4,49]{1,0:T(4,128)}, u32[]{:S(2)}) copy-start(s32[4,49]{1,0:T(4,128)} %param.20) | copy-start | bytes 2356
  197.0 44.4 %copy-start.6 = (f32[1024]{0:T(1024)S(1)}, f32[1024]{0:T(1024)}, u32[]{:S(2)}) copy-start(f32[1024]{0:T(1024)} %param.25) | copy-start | bytes 12292
  198.3 44.3 %copy-start.1 = (bf16[512,512]{1,0:T(8,128)(2,1)S(1)}, bf16[512,512]{1,0:T(8,128)(2,1)}, u32[]{:S(2)}) copy-start(bf16[512,512]{1,0:T(8,128)(2,1)} %param.31) | copy-start | bytes 1572868
  198.3 44.3 %copy-start.2 = (f32[512]{0:T(512)S(1)}, f32[512]{0:T(512)}, u32[]{:S(2)}) copy-start(f32[512]{0:T(512)} %param.29) | copy-start | bytes 6148
  198.3 44.3 %copy-start.3 = (bf16[512]{0:T(512)(128)(2,1)S(1)}, bf16[512]{0:T(512)(128)(2,1)}, u32[]{:S(2)}) copy-start(bf16[512]{0:T(512)(128)(2,1)} %param.27) | copy-start | bytes 3076
  198.3 42.3 %all-to-all-start.2 = ((bf16[16,24,1024]{2,1,0:T(8,128)(2,1)}), bf16[16,24,1024]{2,1,0:T(8,128)(2,1)S(1)}, u32[]{:S(2)}, u32[]{:S(2)}) async-start(bf16[16,24,1024]{2,1,0:T(8,128)(2,1)} %copy.52), calls=%async_computation.2 | async-start | bytes 1572864 | tf_op jit(solution)/shard_map/all_to_all | solution.py:129
Sparse Core Ops, SparseCore 0:
  10.5 90.6 all-gather.4
  104.4 84.8 all-gather.6
where the time goes:
time: 294 us; the launch traced here: 293 us
  waiting for transfers between devices  101 us (34%)
  blocking collectives  83.8 us (29%)
  matrix products  50.2 us (17%)
  starting transfers between devices  25.2 us (9%)
  between operations  16.2 us (6%)
  local copies, waits for them, and re-layouts  9.71 us (3%)
  other arithmetic  6.8 us (2%)
    all_gather x1, waiting for transfers between devices, per_device(): piece_out = lax.all_gather(expert_out, 'dp', axis=1, tiled=True)  88 us
    unnamed x1, blocking collectives  55.7 us
    all_gather x1, blocking collectives, per_device(): lax.all_gather(visible, 'expert', axis=0, tiled=True)  28.1 us
    sub x4, matrix products, decode_image(): raised = jnp.exp(scores - highest)  12 us
    all_to_all x1, starting transfers between devices, per_device(): lax.all_to_all(outgoing, 'expert', split_axis=0, concat_axis=0, tiled=True)  10.9 us
    all_to_all x1, starting transfers between devices, per_device(): lax.all_to_all(send_weight.reshape(groups, exp_dev * capacity), 'expert',...  10.1 us
    dot_general x4, matrix products, decode_image(): jnp.einsum('ihqk,ikhc->iqhc', weights, value_rows, preferred_element_type...  9.58 us
    dot_general x4, matrix products, decode_image(): jnp.dot(dec_normed.reshape(GRID, DD), attention_in, preferred_element_typ...  7.77 us
  transfers between devices with their start and end apart: 5, of which 3 were waited for; matrix products, arithmetic and copies ran while one was open for 4% of the time, Pallas kernels for 0%

commit v1 on v0

--- a/solution.py
+++ b/solution.py
@@ -10,6 +10,22 @@
 GRID = 196
 VIS = 49
 EPSILON = 1e-06
+
+
+def gather_around(x, axis, dim):
+    ways, here, step = (lax.axis_size(axis), lax.axis_index(axis), x.shape[dim])
+    shape = [n * ways if d == dim else n for d, n in enumerate(x.shape)]
+    full = lax.dynamic_update_slice_in_dim(jnp.zeros(shape, x.dtype), x, here * step, axis=dim)
+    going_up = going_down = x
+    for far in range(1, ways // 2 + 1):
+        going_up = lax.ppermute(going_up, axis, [(d, (d + 1) % ways) for d in range(ways)])
+        full = lax.dynamic_update_slice_in_dim(full, going_up, (here - far) % ways * step, axis=dim)
+        if 2 * far < ways:
+            going_down = lax.ppermute(going_down, axis, [(d, (d - 1) % ways) for d in range(ways)])
+            full = lax.dynamic_update_slice_in_dim(
+                full, going_down, (here + far) % ways * step, axis=dim
+            )
+    return full
 
 
 def layer_norm(values, factor):
@@ -64,7 +80,7 @@
     token_expert = expert_ids[:, 0]
     all_ids, all_visible, all_owner = (
         lax.all_gather(token_expert, "expert", axis=0, tiled=True),
-        lax.all_gather(visible, "expert", axis=0, tiled=True),
+        gather_around(visible, "expert", 0),
         lax.all_gather(owner_map, "expert", axis=0, tiled=True),
     )
     placing = slot_table(token_expert, experts, capacity)

time: 294 us -> 297 us (1.010)
  blocking collectives: 83.8 us -> 45.9 us
  starting transfers between devices: 25.2 us -> 46.2 us
  waiting for transfers between devices: 101 us -> 118 us
    ppermute x0 -> x15, waiting for transfers between devices: none -> 36.6 us  [the longest x8 30.1 us: gather_around(): lax.ppermute(going_up, axis, [(d, (d + 1) % ways) for d in range(ways)])]
    all_gather x1 -> x0, blocking collectives: 28.1 us -> none  [per_device(): lax.all_gather(visible, 'expert', axis=0, tiled=True)]
    ppermute x0 -> x15, starting transfers between devices: none -> 20.1 us  [the longest x8 13.2 us: gather_around(): lax.ppermute(going_up, axis, [(d, (d + 1) % ways) for d in range(ways)])]
    all_gather x1, waiting for transfers between devices: 88 us -> 77.2 us  [per_device(): piece_out = lax.all_gather(expert_out, 'dp', axis=1, tiled=True)]
    unnamed x1, blocking collectives: 55.7 us -> 45.9 us
    all_gather x1, waiting for transfers between devices: 7.14 us -> 0.02 us  [per_device(): piece_in = lax.all_gather(expert_in, 'dp', axis=1, tiled=True)]
    all_to_all x1, starting transfers between devices: 4.19 us -> 9.02 us  [per_device(): lax.all_to_all(send_rows.reshape(groups, exp_dev * capacity, D), 'expert'...]
    all_to_all x1, waiting for transfers between devices: 4.69 us -> 0.01 us  [per_device(): lax.all_to_all(send_weight.reshape(groups, exp_dev * capacity), 'expert',...]
  transfers between devices with their start and end apart: 5 -> 20, of which waited for: 3 -> 13; matrix products, arithmetic and copies ran while one was open for 4% -> 7% of each run, Pallas kernels for 0% -> 0%
where the time goes in v1:
time: 297 us; the launch traced here: 295 us
  waiting for transfers between devices  118 us (40%)
  matrix products  50.2 us (17%)
  starting transfers between devices  46.2 us (16%)
  blocking collectives  45.9 us (15%)
  between operations  16.1 us (5%)
  local copies, waits for them, and re-layouts  11.1 us (4%)
  other arithmetic  6.71 us (2%)
    all_gather x1, waiting for transfers between devices, per_device(): piece_out = lax.all_gather(expert_out, 'dp', axis=1, tiled=True)  77.2 us
    unnamed x1, blocking collectives  45.9 us
    ppermute x8, waiting for transfers between devices, gather_around(): lax.ppermute(going_up, axis, [(d, (d + 1) % ways) for d in range(ways)])  30.1 us
    ppermute x8, starting transfers between devices, gather_around(): lax.ppermute(going_up, axis, [(d, (d + 1) % ways) for d in range(ways)])  13.2 us
    sub x4, matrix products, decode_image(): raised = jnp.exp(scores - highest)  12 us
    all_to_all x1, starting transfers between devices, per_device(): lax.all_to_all(outgoing, 'expert', split_axis=0, concat_axis=0, tiled=True)  10.9 us
    dot_general x4, matrix products, decode_image(): jnp.einsum('ihqk,ikhc->iqhc', weights, value_rows, preferred_element_type...  9.58 us
    all_to_all x1, starting transfers between devices, per_device(): lax.all_to_all(send_rows.reshape(groups, exp_dev * capacity, D), 'expert'...  9.02 us
  transfers between devices with their start and end apart: 20, of which 13 were waited for; matrix products, arithmetic and copies ran while one was open for 7% of the time, Pallas kernels for 0%

profile of v1, /device:TPU:1, one launch (start us, length us, event | category | flops | bytes accessed | tf_op | source)
XLA Modules:
  0.0 294.5 jit_solution(17449899454444884626)
XLA Ops:
  8.0 2.7 collective-permute-start
  10.7 4.2 %collective-permute-start.1 = (s32[4,49]{1,0:T(4,128)}, s32[4,49]{1,0:T(4,128)S(1)}, u32[]{:S(2)}, u32[]{:S(2)}) collective-permute-start(s32[4,49]{1,0:T(4,128)} %param.20), channel_id=1, source_target_pairs={{0,15},{1,0},{2,1},{3,2},{4,3},{5,4},{6,5},{7,6},{8,7},{9,8},{10,9... | collective-permute-start | bytes 2360 | tf_op jit(solution)/shard_map/ppermute | solution.py:24
  19.5 6.1 %all-to-all-start.1 = ((bf16[16,1,24]{2,1,0:T(2,128)(2,1)}), bf16[16,1,24]{2,1,0:T(2,128)(2,1)S(1)}, u32[]{:S(2)}, u32[]{:S(2)}) async-start(bf16[16,1,24]{2,1,0:T(2,128)(2,1)} %all_to_all.16), calls=%async_computation.1 | async-start | bytes 16384 | tf_op jit(solution)/shard_map/all_to_all | solution.py:99
  29.9 45.9 %all-reduce.4 = (s32[64]{0:T(128)S(1)}, s32[3136]{0:T(1024)S(1)}) all-reduce(s32[64]{0:T(128)S(1)} %dynamic-update-slice, s32[3136]{0:T(1024)S(1)} %dynamic-update-slice.1), channel_id=1, replica_groups=mesh['dp'=32,'expert'=16] {'expert'}, use_global_device_ids=true, to_apply=%add.2 | all-reduce | flops 3200 | bytes 25600
  79.0 9.0 %all-to-all-start = ((bf16[16,24,1024]{2,1,0:T(8,128)(2,1)}), bf16[16,24,1024]{2,1,0:T(8,128)(2,1)S(1)}, u32[]{:S(2)}, u32[]{:S(2)}) async-start(bf16[16,24,1024]{2,1,0:T(8,128)(2,1)} %bitcast.20), calls=%async_computation | async-start | bytes 1572864 | tf_op jit(solution)/shard_map/all_to_all | solution.py:92
  92.1 11.2 %collective-permute-done.2 = s32[4,49]{1,0:T(4,128)S(1)} collective-permute-done((s32[4,49]{1,0:T(4,128)S(1)}, s32[4,49]{1,0:T(4,128)S(1)}, u32[]{:S(2)}, u32[]{:S(2)}) %collective-permute-start.2) | collective-permute-done | bytes 816 | tf_op jit(solution)/shard_map/ppermute | solution.py:21
  103.3 2.7 collective-permute-start.4
  107.7 3.0 %all-to-all-done = bf16[16,24,1024]{2,1,0:T(8,128)(2,1)S(1)} async-done(((bf16[16,24,1024]{2,1,0:T(8,128)(2,1)}), bf16[16,24,1024]{2,1,0:T(8,128)(2,1)S(1)}, u32[]{:S(2)}, u32[]{:S(2)}) %all-to-all-start) | async-done | bytes 786464 | tf_op jit(solution)/shard_map/all_to_all | solution.py:92
  111.9 77.2 %all-gather.6.cloned.1.call-done = bf16[1,2048,1024]{2,1,0:T(8,128)(2,1)} async-done(((bf16[1,64,1024]{2,1,0:T(8,128)(2,1)}), bf16[1,2048,1024]{2,1,0:T(8,128)(2,1)}) %all-gather.6.cloned.1.call-update) | async-done | bytes 4194320 | tf_op jit(solution)/shard_map/all_gather | solution.py:119
  189.1 7.1 %fusion.42 = bf16[384,1024]{1,0:T(8,128)(2,1)S(1)} fusion(bf16[1,2048,1024]{2,1,0:T(8,128)(2,1)} %all-gather.6.cloned.1.call-done, bf16[384,1024]{1,0:T(8,128)(2,1)S(1)} %bitcast.148, bf16[1,2048,1024]{2,1,0:T(8,128)(2,1)} %all-gather.4.cloned.1.call-done, bf16[16,24,1024]{2,1,0:T(8,128)(2,1)S(1)} %all-to-all-done, f32[384]{0:T(512)S(1)} %reshape.421), kind=kOutput, calls=%fused_computation.55 | convolution fusion | flops 3229876224 | bytes 10749440 | tf_op jit(solution)/shard_map/esf,efd->esd/dot_general | solution.py:123
  198.2 10.9 %all-to-all-start.2 = ((bf16[16,24,1024]{2,1,0:T(8,128)(2,1)}), bf16[16,24,1024]{2,1,0:T(8,128)(2,1)S(1)}, u32[]{:S(2)}, u32[]{:S(2)}) async-start(bf16[16,24,1024]{2,1,0:T(8,128)(2,1)} %copy.52), calls=%async_computation.2 | async-start | bytes 1572864 | tf_op jit(solution)/shard_map/all_to_all | solution.py:145
  210.8 13.6 %collective-permute-done.6 = s32[4,49]{1,0:T(4,128)S(1)} collective-permute-done((s32[4,49]{1,0:T(4,128)S(1)}, s32[4,49]{1,0:T(4,128)S(1)}, u32[]{:S(2)}, u32[]{:S(2)}) %collective-permute-start.6) | collective-permute-done | bytes 816 | tf_op jit(solution)/shard_map/ppermute | solution.py:21
  224.4 2.7 collective-permute-start.8
  238.1 3.7 %collective-permute-done.14 = s32[4,49]{1,0:T(4,128)S(1)} collective-permute-done((s32[4,49]{1,0:T(4,128)S(1)}, s32[4,49]{1,0:T(4,128)S(1)}, u32[]{:S(2)}, u32[]{:S(2)}) %collective-permute-start.14) | collective-permute-done | bytes 816 | tf_op jit(solution)/shard_map/ppermute | solution.py:21
  243.9 41.3 %while.10 = (s32[]{:T(128)}, bf16[4,1,196,512]{3,2,1,0:T(8,128)(2,1)}, s32[4,1,49]{2,1,0:T(1,128)S(1)}, bf16[4,1,49,512]{3,2,1,0:T(8,128)(2,1)}, bf16[512]{0:T(5...) while((s32[]{:T(128)}, ...), condition=%wide.region_17.18_spmd, body=%wide.region_11.17_spmd.sunk | while | flops 504361024 | bytes 12126609 | solution.py:189
  247.9 3.0 %fusion.93 = (f32[16,196]{1,0:T(8,128)S(1)}, f32[16,196,196]{1,2,0:T(8,128)}) fusion(bf16[1,196,3,16,32]{1,4,3,2,0:T(8,128)(2,1)S(1)} %bitcast.143), kind=kOutput, calls=%fused_computation.131.clone.1 | convolution fusion | flops 41182148 | bytes 2995456 | tf_op jit(solution)/shard_map/while/body/eval_jaxpr/sub | solution.py:179
  250.8 2.4 fusion.94
  258.2 3.0 %fusion.93 = (f32[16,196]{1,0:T(8,128)S(1)}, f32[16,196,196]{1,2,0:T(8,128)}) fusion(bf16[1,196,3,16,32]{1,4,3,2,0:T(8,128)(2,1)S(1)} %bitcast.143), kind=kOutput, calls=%fused_computation.131.clone.1 | convolution fusion | flops 41182148 | bytes 2995456 | tf_op jit(solution)/shard_map/while/body/eval_jaxpr/sub | solution.py:179
  261.2 2.4 fusion.94
  268.5 3.0 %fusion.93 = (f32[16,196]{1,0:T(8,128)S(1)}, f32[16,196,196]{1,2,0:T(8,128)}) fusion(bf16[1,196,3,16,32]{1,4,3,2,0:T(8,128)(2,1)S(1)} %bitcast.143), kind=kOutput, calls=%fused_computation.131.clone.1 | convolution fusion | flops 41182148 | bytes 2995456 | tf_op jit(solution)/shard_map/while/body/eval_jaxpr/sub | solution.py:179
  271.5 2.4 fusion.94
  278.8 3.0 %fusion.93 = (f32[16,196]{1,0:T(8,128)S(1)}, f32[16,196,196]{1,2,0:T(8,128)}) fusion(bf16[1,196,3,16,32]{1,4,3,2,0:T(8,128)(2,1)S(1)} %bitcast.143), kind=kOutput, calls=%fused_computation.131.clone.1 | convolution fusion | flops 41182148 | bytes 2995456 | tf_op jit(solution)/shard_map/while/body/eval_jaxpr/sub | solution.py:179
  281.8 2.4 fusion.94
  285.2 2.4 copy.67
  (152 shorter events, 54.2 us)
Async XLA Ops:
  6.5 236.1 %copy-start = (bf16[1024,512]{1,0:T(8,128)(2,1)S(1)}, bf16[1024,512]{1,0:T(8,128)(2,1)}, u32[]{:S(2)}) copy-start(bf16[1024,512]{1,0:T(8,128)(2,1)} %param.26) | copy-start | bytes 3145732
  6.5 83.6 %copy-start.6 = (s32[4,49]{1,0:T(4,128)S(1)}, s32[4,49]{1,0:T(4,128)}, u32[]{:S(2)}) copy-start(s32[4,49]{1,0:T(4,128)} %param.20) | copy-start | bytes 2356
  6.5 105.3 %all-gather.4.cloned.1.call-start = ((), (), s32[]{:S(2)}) async-start(), calls=%async_computation.3 | async-start | bytes 4325376 | tf_op jit(solution)/shard_map/all_gather | solution.py:118
  7.3 181.8 %all-gather.6.cloned.1.call-start = ((), (), s32[]{:S(2)}) async-start(), calls=%async_computation.4 | async-start | bytes 4325376 | tf_op jit(solution)/shard_map/all_gather | solution.py:119
  8.0 82.3 %collective-permute-start = (s32[4,49]{1,0:T(4,128)}, s32[4,49]{1,0:T(4,128)S(1)}, u32[]{:S(2)}, u32[]{:S(2)}) collective-permute-start(s32[4,49]{1,0:T(4,128)} %param.20), channel_id=1, source_target_pairs={{0,1},{1,2},{2,3},{3,4},{4,5},{5,6},{6,7},{7,8},{8,9},{9,10},{10,1... | collective-permute-start | bytes 2360 | tf_op jit(solution)/shard_map/ppermute | solution.py:21
  10.7 81.3 %collective-permute-start.1 = (s32[4,49]{1,0:T(4,128)}, s32[4,49]{1,0:T(4,128)S(1)}, u32[]{:S(2)}, u32[]{:S(2)}) collective-permute-start(s32[4,49]{1,0:T(4,128)} %param.20), channel_id=1, source_target_pairs={{0,15},{1,0},{2,1},{3,2},{4,3},{5,4},{6,5},{7,6},{8,7},{9,8},{10,9... | collective-permute-start | bytes 2360 | tf_op jit(solution)/shard_map/ppermute | solution.py:24
  19.5 59.5 %all-to-all-start.1 = ((bf16[16,1,24]{2,1,0:T(2,128)(2,1)}), bf16[16,1,24]{2,1,0:T(2,128)(2,1)S(1)}, u32[]{:S(2)}, u32[]{:S(2)}) async-start(bf16[16,1,24]{2,1,0:T(2,128)(2,1)} %all_to_all.16), calls=%async_computation.1 | async-start | bytes 16384 | tf_op jit(solution)/shard_map/all_to_all | solution.py:99
  79.0 31.7 %all-to-all-start = ((bf16[16,24,1024]{2,1,0:T(8,128)(2,1)}), bf16[16,24,1024]{2,1,0:T(8,128)(2,1)S(1)}, u32[]{:S(2)}, u32[]{:S(2)}) async-start(bf16[16,24,1024]{2,1,0:T(8,128)(2,1)} %bitcast.20), calls=%async_computation | async-start | bytes 1572864 | tf_op jit(solution)/shard_map/all_to_all | solution.py:92
  90.3 13.0 %collective-permute-start.2 = (s32[4,49]{1,0:T(4,128)S(1)}, s32[4,49]{1,0:T(4,128)S(1)}, u32[]{:S(2)}, u32[]{:S(2)}) collective-permute-start(s32[4,49]{1,0:T(4,128)S(1)} %collective-permute-done), channel_id=1, source_target_pairs={{0,1},{1,2},{2,3},{3,4},{4,5},{5,6},{6,7},{7,8},{8,9},{9,10},{10,1... | collective-permute-start | bytes 2360 | tf_op jit(solution)/shard_map/ppermute | solution.py:21
  92.0 15.7 %collective-permute-start.3 = (s32[4,49]{1,0:T(4,128)S(1)}, s32[4,49]{1,0:T(4,128)S(1)}, u32[]{:S(2)}, u32[]{:S(2)}) collective-permute-start(s32[4,49]{1,0:T(4,128)S(1)} %collective-permute-done.1), channel_id=1, source_target_pairs={{0,15},{1,0},{2,1},{3,2},{4,3},{5,4},{6,5},{7,6},{8,7},{9,8},{10,9... | collective-permute-start | bytes 2360 | tf_op jit(solution)/shard_map/ppermute | solution.py:24
  103.3 105.8 %collective-permute-start.4 = (s32[4,49]{1,0:T(4,128)S(1)}, s32[4,49]{1,0:T(4,128)S(1)}, u32[]{:S(2)}, u32[]{:S(2)}) collective-permute-start(s32[4,49]{1,0:T(4,128)S(1)} %collective-permute-done.2), channel_id=1, source_target_pairs={{0,1},{1,2},{2,3},{3,4},{4,5},{5,6},{6,7},{7,8},{8,9},{9,10},{10,1... | collective-permute-start | bytes 2360 | tf_op jit(solution)/shard_map/ppermute | solution.py:21
  107.7 103.1 %collective-permute-start.5 = (s32[4,49]{1,0:T(4,128)S(1)}, s32[4,49]{1,0:T(4,128)S(1)}, u32[]{:S(2)}, u32[]{:S(2)}) collective-permute-start(s32[4,49]{1,0:T(4,128)S(1)} %collective-permute-done.3), channel_id=1, source_target_pairs={{0,15},{1,0},{2,1},{3,2},{4,3},{5,4},{6,5},{7,6},{8,7},{9,8},{10,9... | collective-permute-start | bytes 2360 | tf_op jit(solution)/shard_map/ppermute | solution.py:24
  196.8 45.8 %copy-start.5 = (f32[1024]{0:T(1024)S(1)}, f32[1024]{0:T(1024)}, u32[]{:S(2)}) copy-start(f32[1024]{0:T(1024)} %param.25) | copy-start | bytes 12292
  198.2 45.7 %copy-start.3 = (bf16[512]{0:T(512)(128)(2,1)S(1)}, bf16[512]{0:T(512)(128)(2,1)}, u32[]{:S(2)}) copy-start(bf16[512]{0:T(512)(128)(2,1)} %param.27) | copy-start | bytes 3076
  198.2 43.7 %all-to-all-start.2 = ((bf16[16,24,1024]{2,1,0:T(8,128)(2,1)}), bf16[16,24,1024]{2,1,0:T(8,128)(2,1)S(1)}, u32[]{:S(2)}, u32[]{:S(2)}) async-start(bf16[16,24,1024]{2,1,0:T(8,128)(2,1)} %copy.52), calls=%async_computation.2 | async-start | bytes 1572864 | tf_op jit(solution)/shard_map/all_to_all | solution.py:145
  209.2 15.3 %collective-permute-start.6 = (s32[4,49]{1,0:T(4,128)S(1)}, s32[4,49]{1,0:T(4,128)S(1)}, u32[]{:S(2)}, u32[]{:S(2)}) collective-permute-start(s32[4,49]{1,0:T(4,128)S(1)} %collective-permute-done.4), channel_id=1, source_target_pairs={{0,1},{1,2},{2,3},{3,4},{4,5},{5,6},{6,7},{7,8},{8,9},{9,10},{10,1... | collective-permute-start | bytes 2360 | tf_op jit(solution)/shard_map/ppermute | solution.py:21
  210.8 18.0 %collective-permute-start.7 = (s32[4,49]{1,0:T(4,128)S(1)}, s32[4,49]{1,0:T(4,128)S(1)}, u32[]{:S(2)}, u32[]{:S(2)}) collective-permute-start(s32[4,49]{1,0:T(4,128)S(1)} %collective-permute-done.5), channel_id=1, source_target_pairs={{0,15},{1,0},{2,1},{3,2},{4,3},{5,4},{6,5},{7,6},{8,7},{9,8},{10,9... | collective-permute-start | bytes 2360 | tf_op jit(solution)/shard_map/ppermute | solution.py:24
  224.4 4.7 %collective-permute-start.8 = (s32[4,49]{1,0:T(4,128)S(1)}, s32[4,49]{1,0:T(4,128)S(1)}, u32[]{:S(2)}, u32[]{:S(2)}) collective-permute-start(s32[4,49]{1,0:T(4,128)S(1)} %collective-permute-done.6), channel_id=1, source_target_pairs={{0,1},{1,2},{2,3},{3,4},{4,5},{5,6},{6,7},{7,8},{8,9},{9,10},{10,1... | collective-permute-start | bytes 2360 | tf_op jit(solution)/shard_map/ppermute | solution.py:21
  228.8 3.3 %collective-permute-start.9 = (s32[4,49]{1,0:T(4,128)S(1)}, s32[4,49]{1,0:T(4,128)S(1)}, u32[]{:S(2)}, u32[]{:S(2)}) collective-permute-start(s32[4,49]{1,0:T(4,128)S(1)} %collective-permute-done.7), channel_id=1, source_target_pairs={{0,15},{1,0},{2,1},{3,2},{4,3},{5,4},{6,5},{7,6},{8,7},{9,8},{10,9... | collective-permute-start | bytes 2360 | tf_op jit(solution)/shard_map/ppermute | solution.py:24
  229.2 4.2 %collective-permute-start.10 = (s32[4,49]{1,0:T(4,128)S(1)}, s32[4,49]{1,0:T(4,128)S(1)}, u32[]{:S(2)}, u32[]{:S(2)}) collective-permute-start(s32[4,49]{1,0:T(4,128)S(1)} %collective-permute-done.8), channel_id=1, source_target_pairs={{0,1},{1,2},{2,3},{3,4},{4,5},{5,6},{6,7},{7,8},{8,9},{9,10},{10,1... | collective-permute-start | bytes 2360 | tf_op jit(solution)/shard_map/ppermute | solution.py:21
  232.1 3.0 %collective-permute-start.11 = (s32[4,49]{1,0:T(4,128)S(1)}, s32[4,49]{1,0:T(4,128)S(1)}, u32[]{:S(2)}, u32[]{:S(2)}) collective-permute-start(s32[4,49]{1,0:T(4,128)S(1)} %collective-permute-done.9), channel_id=1, source_target_pairs={{0,15},{1,0},{2,1},{3,2},{4,3},{5,4},{6,5},{7,6},{8,7},{9,8},{10,9... | collective-permute-start | bytes 2360 | tf_op jit(solution)/shard_map/ppermute | solution.py:24
  233.4 4.2 %collective-permute-start.12 = (s32[4,49]{1,0:T(4,128)S(1)}, s32[4,49]{1,0:T(4,128)S(1)}, u32[]{:S(2)}, u32[]{:S(2)}) collective-permute-start(s32[4,49]{1,0:T(4,128)S(1)} %collective-permute-done.10), channel_id=1, source_target_pairs={{0,1},{1,2},{2,3},{3,4},{4,5},{5,6},{6,7},{7,8},{8,9},{9,10},{10,1... | collective-permute-start | bytes 2360 | tf_op jit(solution)/shard_map/ppermute | solution.py:21
  235.1 3.0 %collective-permute-start.13 = (s32[4,49]{1,0:T(4,128)S(1)}, s32[4,49]{1,0:T(4,128)S(1)}, u32[]{:S(2)}, u32[]{:S(2)}) collective-permute-start(s32[4,49]{1,0:T(4,128)S(1)} %collective-permute-done.11), channel_id=1, source_target_pairs={{0,15},{1,0},{2,1},{3,2},{4,3},{5,4},{6,5},{7,6},{8,7},{9,8},{10,9... | collective-permute-start | bytes 2360 | tf_op jit(solution)/shard_map/ppermute | solution.py:24
  237.6 4.2 %collective-permute-start.14 = (s32[4,49]{1,0:T(4,128)S(1)}, s32[4,49]{1,0:T(4,128)S(1)}, u32[]{:S(2)}, u32[]{:S(2)}) collective-permute-start(s32[4,49]{1,0:T(4,128)S(1)} %collective-permute-done.12), channel_id=1, source_target_pairs={{0,1},{1,2},{2,3},{3,4},{4,5},{5,6},{6,7},{7,8},{8,9},{9,10},{10,1... | collective-permute-start | bytes 2360 | tf_op jit(solution)/shard_map/ppermute | solution.py:21
  (3 other events, 124.0 us)
Sparse Core Ops, SparseCore 0:
  10.5 90.5 all-gather.3
  104.3 84.7 all-gather.5
